TPU v7x, 32 devices: a whole 2x2x4 slice. The times are simulated.
32 devices in a mesh: owner: 4 (over y, x), batch: 8 (over z, core).
Axes of the slice: x: 2, y: 2, z: 4, core: 2. Of those that a mesh axis runs over, the one named last changes fastest.
Arguments:
- hidden: bfloat16 [512, 6144], P(('owner', 'batch')), may hold values from -6 to 6
- gains: float32 [2, 6144], replicated, may hold values from 0.25 to 1.75
- up_rows: bfloat16 [98304, 6144], P(('owner', 'batch')), may hold values from -0.078125 to 0.078125
- down_rows: bfloat16 [98304, 6144], P(('owner', 'batch')), may hold values from -0.1875 to 0.1875
- pick: int32 [4, 32], replicated, may hold values from 0 to 24, as said below
Outputs:
- final_rows: bfloat16 [512, 6144], P(('owner', 'batch'))
Inputs may be any that keep to these rules, and one draw needn't show every extreme that they name: pick[g, u] names the one block among unit u's 24 blocks that row block g uses, or is 24 when it uses none of them. In every row block there is a lane of which every unit is used, and a unit that is not.
All inputs are finite; a program needn't handle non-finite values.
Results may differ from a plain program's by a relative error of at most 0.018.
Values may be sent and summed in bfloat16 or wider, within the bound.
A program may use at most 192 MiB of HBM per device.

v0:
```python
import jax
import jax.numpy as jnp
from jax import lax
from jax.sharding import PartitionSpec as P

BLOCK = 128
LAYERS = 2


def normalize(rows_in, gain_row):
    values = rows_in.astype(jnp.float32)
    row_mean = jnp.mean(values, axis=1, keepdims=True)
    centered = values - row_mean
    row_var = jnp.mean(centered * centered, axis=1, keepdims=True)
    return (centered * lax.rsqrt(row_var + 1e-05) * gain_row[None, :]).astype(jnp.bfloat16)


def body(hidden, gains, up_rows, down_rows, pick):
    owners = lax.axis_size("owner")
    batches = lax.axis_size("batch")
    group_at = lax.axis_index("owner")
    lane_at = lax.axis_index("batch")
    held_blocks = up_rows.shape[0] // BLOCK
    model_width = up_rows.shape[1]
    local_rows = hidden.shape[0]
    sender = group_at * batches + lane_at
    my_picks = lax.dynamic_slice_in_dim(pick, sender, 1, 1)[:, 0]
    chosen = jnp.minimum(my_picks, held_blocks - 1)
    up_send = up_rows.reshape(held_blocks, BLOCK, model_width)[chosen]
    down_send = down_rows.reshape(held_blocks, BLOCK, model_width)[chosen]
    group_picks = lax.dynamic_slice_in_dim(pick, group_at, 1, 0)[0]
    live_slots = (group_picks[jnp.arange(owners) * batches + lane_at] < held_blocks).astype(
        jnp.float32
    )
    up_recv, down_recv = (
        lax.all_to_all(up_send, "owner", split_axis=0, concat_axis=0, tiled=True),
        lax.all_to_all(down_send, "owner", split_axis=0, concat_axis=0, tiled=True),
    )
    per_layer = owners // LAYERS
    residual = hidden
    for layer_at in range(LAYERS):
        first_slot = layer_at * per_layer
        up_part = up_recv[first_slot : first_slot + per_layer]
        down_part = down_recv[first_slot : first_slot + per_layer]
        keep_slots = live_slots[first_slot : first_slot + per_layer]
        up_flat = up_part.reshape(per_layer * BLOCK, model_width)
        down_flat = down_part.reshape(per_layer * BLOCK, model_width)
        neuron_mask = jnp.repeat(keep_slots, BLOCK)
        normed = normalize(residual, gains[layer_at])

        def expand(
            rows_piece,
            row_start,
            up_part=up_part,
            up_flat=up_flat,
            keep_slots=keep_slots,
            neuron_mask=neuron_mask,
        ):
            pre_act = lax.dot_general(
                rows_piece, up_flat, (((1,), (1,)), ((), ())), preferred_element_type=jnp.float32
            )
            return (jnp.maximum(pre_act, 0.0) * neuron_mask[None, :]).astype(jnp.bfloat16)

        active = expand(lax.all_gather(normed, "batch", axis=0, tiled=True), jnp.int32(0))

        def contract(
            row_start,
            row_count,
            active=active,
            down_part=down_part,
            down_flat=down_flat,
            keep_slots=keep_slots,
        ):
            return jnp.dot(active, down_flat, preferred_element_type=jnp.float32)

        summed = lax.psum_scatter(
            contract(jnp.int32(0), lax.axis_size("batch") * local_rows).astype(jnp.bfloat16),
            "batch",
            scatter_dimension=0,
            tiled=True,
        ).astype(jnp.float32)
        residual = (residual.astype(jnp.float32) + summed).astype(jnp.bfloat16)
    return residual


def solution(mesh):
    in_specs = (
        P(("owner", "batch"), None),
        P(),
        P(("owner", "batch"), None),
        P(("owner", "batch"), None),
        P(),
    )
    out_specs = P(("owner", "batch"), None)
    return jax.shard_map(body, mesh=mesh, in_specs=in_specs, out_specs=out_specs, check_vma=False)
```

profile of v0, /device:TPU:0, one launch (start us, length us, event | category | flops | bytes accessed | tf_op | source)
XLA Modules:
  0.0 287.6 jit_solution(10123158240245625704)
XLA Ops:
  6.5 0.9 fusion.20
  7.4 6.7 %gather_fusion = bf16[4,128,6144]{2,1,0:T(8,128)(2,1)} fusion(bf16[24,128,6144]{2,1,0:T(8,128)(2,1)} %bitcast.24, s32[1024]{0:T(1024)S(1)} %pad_clamp_fusion.1), kind=kCustom, calls=%fused_computation | custom fusion | bytes 12582928 | tf_op jit(solution)/shard_map/gather | solution.py:29
  14.1 5.2 %all-to-all-start = ((bf16[4,128,6144]{2,1,0:T(8,128)(2,1)}), bf16[4,128,6144]{2,1,0:T(8,128)(2,1)}, u32[]{:S(2)}, u32[]{:S(2)}) async-start(bf16[4,128,6144]{2,1,0:T(8,128)(2,1)} %gather_fusion), calls=%async_computation | async-start | bytes 12582912 | tf_op jit(solution)/shard_map/all_to_all | solution.py:36
  19.3 0.0 copy-start
  19.4 6.7 %gather_fusion.2 = bf16[4,128,6144]{2,1,0:T(8,128)(2,1)} fusion(bf16[24,128,6144]{2,1,0:T(8,128)(2,1)} %bitcast.25, s32[1024]{0:T(1024)S(1)} %pad_clamp_fusion.1), kind=kCustom, calls=%fused_computation.2 | custom fusion | bytes 12582928 | tf_op jit(solution)/shard_map/gather | solution.py:30
  26.0 0.0 copy-done
  26.0 0.2 convert_reduce_fusion.1
  26.2 0.2 fusion.11
  26.5 0.0 copy-start.1
  26.5 64.1 %all-to-all-done = bf16[4,128,6144]{2,1,0:T(8,128)(2,1)} async-done(((bf16[4,128,6144]{2,1,0:T(8,128)(2,1)}), bf16[4,128,6144]{2,1,0:T(8,128)(2,1)}, u32[]{:S(2)}, u32[]{:S(2)}) %all-to-all-start) | async-done | bytes 6291488 | tf_op jit(solution)/shard_map/all_to_all | solution.py:36
  90.6 5.2 %all-to-all-start.1 = ((bf16[4,128,6144]{2,1,0:T(8,128)(2,1)}), bf16[4,128,6144]{2,1,0:T(8,128)(2,1)}, u32[]{:S(2)}, u32[]{:S(2)}) async-start(bf16[4,128,6144]{2,1,0:T(8,128)(2,1)} %gather_fusion.2), calls=%async_computation.1 | async-start | bytes 12582912 | tf_op jit(solution)/shard_map/all_to_all | solution.py:37
  95.8 0.0 all-gather.3.cloned.1.call-start
  95.9 0.0 copy-done.1
  95.9 0.6 fusion.27
  96.5 0.8 fusion.13
  97.3 0.0 all-gather.3.cloned.1.call-update
  97.3 0.0 reduce-scatter.3.cloned.1.call-start
  97.4 0.1 fusion.21
  97.5 0.7 dynamic-slice_bitcast_fusion
  98.2 0.6 gather_fusion.1
  98.8 0.1 fusion.28
  98.9 0.1 broadcast_bitcast_fusion.1
  99.0 5.1 %fusion.25 = (bf16[2,128,6144]{2,1,0:T(8,128)(2,1)S(1)}, bf16[2,128,6144]{2,1,0:T(8,128)(2,1)}) fusion(bf16[4,128,6144]{2,1,0:T(8,128)(2,1)} %all-to-all-done), kind=kLoop, calls=%fused_computation.49 | loop fusion | bytes 12582912 | tf_op jit(solution)/shard_map/slice | solution.py:43
  104.1 61.2 %all-to-all-done.1 = bf16[4,128,6144]{2,1,0:T(8,128)(2,1)} async-done(((bf16[4,128,6144]{2,1,0:T(8,128)(2,1)}), bf16[4,128,6144]{2,1,0:T(8,128)(2,1)}, u32[]{:S(2)}, u32[]{:S(2)}) %all-to-all-start.1) | async-done | bytes 6291488 | tf_op jit(solution)/shard_map/all_to_all | solution.py:37
  165.3 6.2 %fusion.26 = (bf16[2,128,6144]{2,1,0:T(8,128)(2,1)}, bf16[2,128,6144]{2,1,0:T(8,128)(2,1)}) fusion(bf16[4,128,6144]{2,1,0:T(8,128)(2,1)} %all-to-all-done.1), kind=kLoop, calls=%fused_computation.50 | loop fusion | bytes 12582912 | tf_op jit(solution)/shard_map/slice | solution.py:44
  171.5 0.0 all-gather.3.cloned.1.call-done
  171.5 6.8 %convolution_convert_fusion.1 = bf16[128,6144]{1,0:T(8,128)(2,1)} fusion(bf16[256,6144]{1,0:T(8,128)(2,1)} %bitcast.23, bf16[128,6144]{1,0:T(8,128)(2,1)} %all-gather.3.cloned.1.call-done, bf16[256,6144]{1,0:T(8,128)(2,1)} %bitcast.22, f32[256]{0:T(256)S(1)} %broadcast_bitcast_fusion.1), kind=kOutput, calls=%fused_computation.4 | convolution fusion | flops 806191104 | bytes 9438208 | tf_op jit(solution)/shard_map/dot_general | solution.py:74
  178.3 0.0 reduce-scatter.3.cloned.1.call-update
  178.3 0.0 all-gather.5.cloned.1.call-start
  178.4 35.0 %reduce-scatter.3.cloned.1.call-done = bf16[16,6144]{1,0:T(8,128)(2,1)} async-done(((bf16[128,6144]{1,0:T(8,128)(2,1)}), bf16[16,6144]{1,0:T(8,128)(2,1)}) %reduce-scatter.3.cloned.1.call-update) | async-done | bytes 196624 | tf_op jit(solution)/shard_map/reduce_scatter | solution.py:76
  213.4 1.1 convert_reduce_fusion
  214.5 0.2 fusion.8
  214.8 1.6 fusion.10
  216.3 0.0 all-gather.5.cloned.1.call-update
  216.4 0.0 reduce-scatter.5.cloned.1.call-start
  216.4 0.1 broadcast_bitcast_fusion
  216.5 23.6 %all-gather.5.cloned.1.call-done = bf16[128,6144]{1,0:T(8,128)(2,1)} async-done(((bf16[16,6144]{1,0:T(8,128)(2,1)}), bf16[128,6144]{1,0:T(8,128)(2,1)}) %all-gather.5.cloned.1.call-update) | async-done | bytes 1572880 | tf_op jit(solution)/shard_map/all_gather | solution.py:64
  240.1 5.8 %convolution_convert_fusion = bf16[128,6144]{1,0:T(8,128)(2,1)} fusion(bf16[256,6144]{1,0:T(8,128)(2,1)} %bitcast.21, bf16[128,6144]{1,0:T(8,128)(2,1)} %all-gather.5.cloned.1.call-done, bf16[256,6144]{1,0:T(8,128)(2,1)S(1)} %bitcast.20, f32[256]{0:T(256)S(1)} %broadcast_bitcast_fusion), kind=kOutput, calls=%fused_computation.3 | convolution fusion | flops 806191104 | bytes 9438208 | tf_op jit(solution)/shard_map/dot_general | solution.py:74
  245.9 0.0 reduce-scatter.5.cloned.1.call-update
  245.9 33.5 %reduce-scatter.5.cloned.1.call-done = bf16[16,6144]{1,0:T(8,128)(2,1)} async-done(((bf16[128,6144]{1,0:T(8,128)(2,1)}), bf16[16,6144]{1,0:T(8,128)(2,1)}) %reduce-scatter.5.cloned.1.call-update) | async-done | bytes 196624 | tf_op jit(solution)/shard_map/reduce_scatter | solution.py:76
  279.5 1.6 fusion.15
  (7 shorter events, 0.0 us)
Async XLA Ops:
  14.1 76.5 %all-to-all-start = ((bf16[4,128,6144]{2,1,0:T(8,128)(2,1)}), bf16[4,128,6144]{2,1,0:T(8,128)(2,1)}, u32[]{:S(2)}, u32[]{:S(2)}) async-start(bf16[4,128,6144]{2,1,0:T(8,128)(2,1)} %gather_fusion), calls=%async_computation | async-start | bytes 12582912 | tf_op jit(solution)/shard_map/all_to_all | solution.py:36
  19.3 6.7 %copy-start = (bf16[16,6144]{1,0:T(8,128)(2,1)S(1)}, bf16[16,6144]{1,0:T(8,128)(2,1)}, u32[]{:S(2)}) copy-start(bf16[16,6144]{1,0:T(8,128)(2,1)} %param.5) | copy-start | bytes 589828
  26.5 69.4 %copy-start.1 = (f32[2,6144]{1,0:T(2,128)S(1)}, f32[2,6144]{1,0:T(2,128)}, u32[]{:S(2)}) copy-start(f32[2,6144]{1,0:T(2,128)} %param.6) | copy-start | bytes 147460
  90.6 74.7 %all-to-all-start.1 = ((bf16[4,128,6144]{2,1,0:T(8,128)(2,1)}), bf16[4,128,6144]{2,1,0:T(8,128)(2,1)}, u32[]{:S(2)}, u32[]{:S(2)}) async-start(bf16[4,128,6144]{2,1,0:T(8,128)(2,1)} %gather_fusion.2), calls=%async_computation.1 | async-start | bytes 12582912 | tf_op jit(solution)/shard_map/all_to_all | solution.py:37
  95.8 75.7 %all-gather.3.cloned.1.call-start = ((), (), s32[]{:S(2)}) async-start(), calls=%async_computation.4 | async-start | bytes 1769472 | tf_op jit(solution)/shard_map/all_gather | solution.py:64
  97.3 116.1 %reduce-scatter.3.cloned.1.call-start = ((), (), s32[]{:S(2)}) async-start(), calls=%async_computation.5 | async-start | bytes 1769472 | tf_op jit(solution)/shard_map/reduce_scatter | solution.py:76
  178.3 61.7 %all-gather.5.cloned.1.call-start = ((), (), s32[]{:S(2)}) async-start(), calls=%async_computation.6 | async-start | bytes 1769472 | tf_op jit(solution)/shard_map/all_gather | solution.py:64
  216.4 63.1 %reduce-scatter.5.cloned.1.call-start = ((), (), s32[]{:S(2)}) async-start(), calls=%async_computation.7 | async-start | bytes 1769472 | tf_op jit(solution)/shard_map/reduce_scatter | solution.py:76
Sparse Core Ops, SparseCore 0:
  98.3 27.3 all-gather.2
  178.5 34.9 reduce-scatter.2
  216.5 23.5 all-gather.4
  246.0 33.3 reduce-scatter.4
where the time goes:
time: 288 us
  waiting for transfers between devices  217 us (75%)
  local copies, waits for them, and re-layouts  26.9 us (9%)
  between operations  13.2 us (5%)
  matrix products  12.6 us (4%)
  starting transfers between devices  10.6 us (4%)
  other arithmetic  6.79 us (2%)
    reduce_scatter x2, waiting for transfers between devices, body(): lax.psum_scatter(contract(jnp.int32(0), lax.axis_size('batch') * local_ro...  68.6 us
    all_to_all x1, waiting for transfers between devices, body(): lax.all_to_all(up_send, 'owner', split_axis=0, concat_axis=0, tiled=True)  64.1 us
    all_to_all x1, waiting for transfers between devices, body(): lax.all_to_all(down_send, 'owner', split_axis=0, concat_axis=0, tiled=True)  61.2 us
    all_gather x2, waiting for transfers between devices, body(): lax.all_gather(normed, 'batch', axis=0, tiled=True)  23.6 us
    dot_general x2, matrix products, contract(): return jnp.dot(active, down_flat, preferred_element_type=jnp.float32)  12.6 us
    gather x1, local copies, waits for them, and re-layouts, body(): up_send = up_rows.reshape(held_blocks, BLOCK, model_width)[chosen]  6.69 us
    gather x1, local copies, waits for them, and re-layouts, body(): down_send = down_rows.reshape(held_blocks, BLOCK, model_width)[chosen]  6.69 us
    slice x1, local copies, waits for them, and re-layouts, body(): down_part = down_recv[first_slot:first_slot + per_layer]  6.25 us
  transfers between devices with their start and end apart: 6, of which 5 were waited for; matrix products, arithmetic and copies ran while one was open for 8% of the time, Pallas kernels for 0%

commit v1 on v0

--- a/solution.py
+++ b/solution.py
@@ -1,10 +1,311 @@
+import functools
+
 import jax
 import jax.numpy as jnp
 from jax import lax
+from jax.experimental import pallas as pl
+from jax.experimental.pallas import tpu as pltpu
 from jax.sharding import PartitionSpec as P
 
 BLOCK = 128
 LAYERS = 2
+CORES = 2
+VMEM_BUDGET = 60 * 1024 * 1024
+CHUNK = 1024
+
+
+def layer_kernel(
+    layer_at, owners, batches,
+    state_ref, gains_ref, live_ref, up_hbm, down_hbm, out_ref,
+    acts, up_v, down_v, part, core_in, x_in, x2_in, y_in, relay_in, z_in,
+    wsem, zs, xs, ps, x2s, ys, yrs, ag_recv,
+    cs, cr, rxs, rx2s, rys, ryrs, rzs, rxr, rx2r, ryr, ryrr, rzr,
+):
+    zn = batches // CORES
+    per_layer = owners // LAYERS
+    rows, width = state_ref.shape
+    half = width // 2
+    me_o = lax.axis_index("owner")
+    me_b = lax.axis_index("batch")
+    hi, lo = me_o // per_layer, me_o % per_layer
+    zi, core = me_b // CORES, me_b % CORES
+    peer_x = hi * per_layer + (1 - lo)
+    peer_y = (1 - hi) * per_layer + lo
+    diag = (1 - hi) * per_layer + (1 - lo)
+    partner = zi * CORES + (1 - core)
+    x_dev, y_dev, p_dev = (peer_x, me_b), (peer_y, me_b), (me_o, partner)
+    in_layer = hi == layer_at
+
+    def at_z(k):
+        return (zi + k) % zn
+
+    def z_dev(k):
+        return (me_o, at_z(k) * CORES + core)
+
+    def slot(z):
+        return z * CORES + core
+
+    def remote(src, dst, ssem, rsem, dev):
+        return pltpu.make_async_remote_copy(
+            src_ref=src, dst_ref=dst, send_sem=ssem, recv_sem=rsem,
+            device_id=dev, device_id_type=pl.DeviceIdType.MESH)
+
+    def piece(o, b, h):
+        return acts.at[o, b, :, pl.ds(h * half, half)]
+
+    def move(o, b, h, ssem, dev):
+        return remote(piece(o, b, h), piece(o, b, h), ssem, ag_recv.at[o, b, h], dev)
+
+    def arrive(o, b, h):
+        move(o, b, h, zs.at[0, h], x_dev).wait_recv()
+
+    @pl.when(in_layer)
+    def _():
+        pltpu.make_async_copy(up_hbm, up_v, wsem.at[0]).start()
+        pltpu.make_async_copy(down_hbm, down_v, wsem.at[1]).start()
+
+    values = state_ref[...].astype(jnp.float32)
+    mean = jnp.mean(values, axis=1, keepdims=True)
+    centered = values - mean
+    var = jnp.mean(centered * centered, axis=1, keepdims=True)
+    acts[me_o, me_b] = (
+        centered * lax.rsqrt(var + 1e-05) * gains_ref[layer_at:layer_at + 1, :]
+    ).astype(jnp.bfloat16)
+
+    barrier = pltpu.get_barrier_semaphore()
+    greeted = [x_dev, y_dev, p_dev] + [z_dev(k) for k in range(1, zn)]
+    for dev in greeted:
+        pl.semaphore_signal(barrier, inc=1, device_id=dev, device_id_type=pl.DeviceIdType.MESH)
+    pl.semaphore_wait(barrier, len(greeted))
+
+    for k in range(1, zn):
+        for h in range(2):
+            move(me_o, me_b, h, zs.at[k, h], z_dev(k)).start()
+
+    @pl.when(in_layer)
+    def _():
+        def to_partner(o, k):
+            for h in range(2):
+                move(o, slot(at_z(k)), h, ps.at[o, k, h], p_dev).start()
+
+        for t in range(zn + 2):
+            if t < zn:
+                b = slot(at_z(t))
+                if t > 0:
+                    for h in range(2):
+                        arrive(me_o, b, h)
+                for h in range(2):
+                    move(me_o, b, h, xs.at[t, h], x_dev).start()
+                to_partner(me_o, t)
+            if 1 <= t <= zn:
+                b = slot(at_z(t - 1))
+                for h in range(2):
+                    arrive(peer_y, b, h)
+                move(peer_y, b, 1, x2s.at[t - 1], x_dev).start()
+                to_partner(peer_y, t - 1)
+            if t >= 2:
+                b = slot(at_z(t - 2))
+                for o in (peer_x, diag):
+                    for h in range(2):
+                        arrive(o, b, h)
+                    to_partner(o, t - 2)
+
+        for g in range(owners):
+            for k in range(zn):
+                for h in range(2):
+                    arrive(g, at_z(k) * CORES + (1 - core), h)
+        pltpu.make_async_copy(up_hbm, up_v, wsem.at[0]).wait()
+        pltpu.make_async_copy(down_hbm, down_v, wsem.at[1]).wait()
+
+        def give(g, k):
+            z = at_z(k)
+            return remote(part.at[g, z * CORES + (1 - core)], core_in.at[g, z], cs.at[g, k], cr.at[g, z], p_dev)
+
+        def group(g, carry):
+            flat = acts[g].reshape(batches * rows, width)
+            pre = lax.dot_general(flat, up_v[g], (((1,), (1,)), ((), ())), preferred_element_type=jnp.float32)
+            active = (jnp.maximum(pre, 0.0) * live_ref[pl.ds(g, 1), :]).astype(jnp.bfloat16)
+            for at in range(0, width, CHUNK):
+                cols = pl.ds(at, min(CHUNK, width - at))
+                made = jnp.dot(active, down_v[g, :, cols], preferred_element_type=jnp.float32)
+                part[g, :, :, cols] = made.astype(jnp.bfloat16).reshape(batches, rows, -1)
+            for k in range(zn):
+                give(g, k).start()
+            return carry
+
+        lax.fori_loop(0, owners, group, 0)
+
+        def join(g, z, b):
+            remote(part.at[g, b], core_in.at[g, z], cs.at[g, 0], cr.at[g, z], p_dev).wait_recv()
+            core_in[g, z] = (core_in[g, z].astype(jnp.float32) + part[g, b].astype(jnp.float32)).astype(jnp.bfloat16)
+
+        h2 = pl.ds(half, half)
+        h1 = pl.ds(0, half)
+        for k in range(zn):
+            z = at_z(k)
+            join(diag, z, slot(z))
+            remote(core_in.at[diag, z, :, h2], x2_in.at[z], rx2s.at[k], rx2r.at[z], x_dev).start()
+            remote(core_in.at[diag, z, :, h1], relay_in.at[z], ryrs.at[k], ryrr.at[z], y_dev).start()
+        for k in range(zn):
+            z = at_z(k)
+            join(peer_y, z, slot(z))
+            remote(core_in.at[peer_y, z, :, h1], y_in.at[z, :, h1], rys.at[k, 0], ryr.at[z, 0], y_dev).start()
+            join(peer_x, z, slot(z))
+            remote(core_in.at[peer_x, z], x_in.at[z], rxs.at[k], rxr.at[z], x_dev).start()
+        for k in range(zn):
+            z = at_z(k)
+            remote(core_in.at[diag, z, :, h2], x2_in.at[z], rx2s.at[k], rx2r.at[z], x_dev).wait_recv()
+            core_in[peer_y, z, :, half:] = (
+                core_in[peer_y, z, :, half:].astype(jnp.float32) + x2_in[z].astype(jnp.float32)
+            ).astype(jnp.bfloat16)
+            remote(core_in.at[peer_y, z, :, h2], y_in.at[z, :, h2], rys.at[k, 1], ryr.at[z, 1], y_dev).start()
+        for k in list(range(1, zn)) + [0]:
+            z = at_z(k)
+            join(me_o, z, slot(z))
+            remote(core_in.at[peer_x, z], x_in.at[z], rxs.at[k], rxr.at[z], x_dev).wait_recv()
+            x_in[z] = (x_in[z].astype(jnp.float32) + core_in[me_o, z].astype(jnp.float32)).astype(jnp.bfloat16)
+            if k:
+                remote(x_in.at[z], z_in.at[zi], rzs.at[k], rzr.at[zi], z_dev(k)).start()
+        out_ref[...] = x_in[zi]
+
+        for k in range(zn):
+            z = at_z(k)
+            for h in range(2):
+                move(me_o, slot(z), h, xs.at[k, h], x_dev).wait_send()
+                for o in range(owners):
+                    move(o, slot(z), h, ps.at[o, k, h], p_dev).wait_send()
+            move(peer_y, slot(z), 1, x2s.at[k], x_dev).wait_send()
+            for g in range(owners):
+                give(g, k).wait_send()
+            remote(core_in.at[diag, z, :, h2], x2_in.at[z], rx2s.at[k], rx2r.at[z], x_dev).wait_send()
+            remote(core_in.at[diag, z, :, h1], relay_in.at[z], ryrs.at[k], ryrr.at[z], y_dev).wait_send()
+            remote(core_in.at[peer_x, z], x_in.at[z], rxs.at[k], rxr.at[z], x_dev).wait_send()
+            remote(core_in.at[peer_y, z, :, h1], y_in.at[z, :, h1], rys.at[k, 0], ryr.at[z, 0], y_dev).wait_send()
+            remote(core_in.at[peer_y, z, :, h2], y_in.at[z, :, h2], rys.at[k, 1], ryr.at[z, 1], y_dev).wait_send()
+
+    @pl.when(jnp.logical_not(in_layer))
+    def _():
+        for t in range(zn + 1):
+            if t < zn:
+                b = slot(at_z(t))
+                if t > 0:
+                    for h in range(2):
+                        arrive(me_o, b, h)
+                move(me_o, b, 0, xs.at[t, 0], x_dev).start()
+                for h in range(2):
+                    move(me_o, b, h, ys.at[t, h], y_dev).start()
+            if t >= 1:
+                b = slot(at_z(t - 1))
+                arrive(peer_x, b, 0)
+                move(peer_x, b, 0, yrs.at[t - 1], y_dev).start()
+
+        h2 = pl.ds(half, half)
+        h1 = pl.ds(0, half)
+
+        def pass_on(k, z):
+            return remote(relay_in.at[z], x2_in.at[z], ryrs.at[k], rx2r.at[z], x_dev)
+
+        order = list(range(1, zn)) + [0]
+        for k in range(zn):
+            z = at_z(k)
+            remote(relay_in.at[z], relay_in.at[z], ryrs.at[k], ryrr.at[z], y_dev).wait_recv()
+            pass_on(k, z).start()
+        for k in order:
+            z = at_z(k)
+            remote(y_in.at[z, :, h1], y_in.at[z, :, h1], rys.at[k, 0], ryr.at[z, 0], y_dev).wait_recv()
+            pass_on(k, z).wait_recv()
+            y_in[z, :, :half] = (y_in[z, :, :half].astype(jnp.float32) + x2_in[z].astype(jnp.float32)).astype(jnp.bfloat16)
+            remote(y_in.at[z, :, h2], y_in.at[z, :, h2], rys.at[k, 1], ryr.at[z, 1], y_dev).wait_recv()
+            if k:
+                remote(y_in.at[z], z_in.at[zi], rzs.at[k], rzr.at[zi], z_dev(k)).start()
+        out_ref[...] = y_in[zi]
+
+        for k in range(zn):
+            z = at_z(k)
+            b = slot(z)
+            move(me_o, b, 0, xs.at[k, 0], x_dev).wait_send()
+            for h in range(2):
+                move(me_o, b, h, ys.at[k, h], y_dev).wait_send()
+            move(peer_x, b, 0, yrs.at[k], y_dev).wait_send()
+            pass_on(k, z).wait_send()
+
+    total = values + out_ref[...].astype(jnp.float32)
+    for k in range(1, zn):
+        z = at_z(k)
+        remote(x_in.at[z], z_in.at[z], rzs.at[k], rzr.at[z], z_dev(k)).wait_recv()
+        total = total + z_in[z].astype(jnp.float32)
+    out_ref[...] = total.astype(jnp.bfloat16)
+    for k in range(1, zn):
+        for h in range(2):
+            move(me_o, me_b, h, zs.at[k, h], z_dev(k)).wait_send()
+        remote(x_in.at[at_z(k)], z_in.at[zi], rzs.at[k], rzr.at[zi], z_dev(k)).wait_send()
+
+
+def scratch_plan(owners, batches, rows, width):
+    zn = batches // CORES
+    half = width // 2
+    bf = jnp.bfloat16
+    return [
+        ((owners, batches, rows, width), bf),
+        ((owners, BLOCK, width), bf),
+        ((owners, BLOCK, width), bf),
+        ((owners, batches, rows, width), bf),
+        ((owners, zn, rows, width), bf),
+        ((zn, rows, width), bf),
+        ((zn, rows, half), bf),
+        ((zn, rows, width), bf),
+        ((zn, rows, half), bf),
+        ((zn, rows, width), bf),
+    ]
+
+
+def scratch_bytes(plan):
+    total = 0
+    for shape, kind in plan:
+        size = jnp.dtype(kind).itemsize
+        for extent in shape:
+            size *= extent
+        total += size
+    return total
+
+
+def run_layer(layer_at, owners, batches, state, gains, live, up_send, down_send):
+    rows, width = state.shape
+    zn = batches // CORES
+    plan = scratch_plan(owners, batches, rows, width)
+    dma = pltpu.SemaphoreType.DMA
+    sems = [(2,), (zn, 2), (zn, 2), (owners, zn, 2), (zn,), (zn, 2), (zn,), (owners, batches, 2),
+            (owners, zn), (owners, zn), (zn,), (zn,), (zn, 2), (zn,), (zn,),
+            (zn,), (zn,), (zn, 2), (zn,), (zn,)]
+    vmem = pl.BlockSpec(memory_space=pltpu.VMEM)
+    hbm = pl.BlockSpec(memory_space=pl.ANY)
+    return pl.pallas_call(
+        functools.partial(layer_kernel, layer_at, owners, batches),
+        out_shape=jax.ShapeDtypeStruct((rows, width), jnp.bfloat16),
+        in_specs=[vmem, vmem, vmem, hbm, hbm],
+        out_specs=vmem,
+        scratch_shapes=[pltpu.VMEM(s, d) for s, d in plan] + [dma(s) for s in sems],
+        compiler_params=pltpu.CompilerParams(
+            collective_id=layer_at, has_side_effects=True, vmem_limit_bytes=VMEM_BUDGET),
+        name=f"sublayer_{layer_at}",
+    )(state, gains, live, up_send, down_send)
+
+
+def stay_body(hidden, gains, up_rows, down_rows, pick):
+    owners = lax.axis_size("owner")
+    batches = lax.axis_size("batch")
+    held_blocks = up_rows.shape[0] // BLOCK
+    model_width = up_rows.shape[1]
+    sender = lax.axis_index("owner") * batches + lax.axis_index("batch")
+    my_picks = lax.dynamic_slice_in_dim(pick, sender, 1, 1)[:, 0]
+    chosen = jnp.minimum(my_picks, held_blocks - 1)
+    up_send = up_rows.reshape(held_blocks, BLOCK, model_width)[chosen]
+    down_send = down_rows.reshape(held_blocks, BLOCK, model_width)[chosen]
+    live = jnp.broadcast_to((my_picks < held_blocks).astype(jnp.float32)[:, None], (owners, BLOCK))
+    state = hidden
+    for layer_at in range(LAYERS):
+        state = run_layer(layer_at, owners, batches, state, gains, live, up_send, down_send)
+    return state
 
 
 def normalize(rows_in, gain_row):
@@ -92,4 +393,14 @@
         P(),
     )
     out_specs = P(("owner", "batch"), None)
-    return jax.shard_map(body, mesh=mesh, in_specs=in_specs, out_specs=out_specs, check_vma=False)
+    owners, batches = mesh.shape["owner"], mesh.shape["batch"]
+
+    def whole(hidden, gains, up_rows, down_rows, pick):
+        rows = hidden.shape[0] // (owners * batches)
+        plan = scratch_plan(owners, batches, rows, hidden.shape[1])
+        fits = owners == 2 * LAYERS and scratch_bytes(plan) * 5 < VMEM_BUDGET * 4
+        chosen = stay_body if fits else body
+        return jax.shard_map(chosen, mesh=mesh, in_specs=in_specs, out_specs=out_specs, check_vma=False)(
+            hidden, gains, up_rows, down_rows, pick)
+
+    return whole

time: 288 us -> 209 us (0.73)
  waiting for transfers between devices: 217 us -> 0 us
  Pallas kernels: 0 us -> 191 us
  between operations: 13.2 us -> 0.02 us
  matrix products: 12.6 us -> 0 us
  local copies, waits for them, and re-layouts: 26.9 us -> 15.3 us
  starting transfers between devices: 10.6 us -> 0 us
  other arithmetic: 6.79 us -> 1.74 us
    pallas_call x0 -> x2, Pallas kernels: none -> 191 us  [run_layer(): pl.pallas_call(functools.partial(layer_kernel, layer_at, owners, batches)...]
    all_to_all x2 -> x0, waiting for transfers between devices: 125 us -> none  [the longest x1 64.1 us: body(): lax.all_to_all(up_send, 'owner', split_axis=0, concat_axis=0, tiled=True)]
    reduce_scatter x2 -> x0, waiting for transfers between devices: 68.6 us -> none  [body(): lax.psum_scatter(contract(jnp.int32(0), lax.axis_size('batch') * local_ro...]
    all_gather x2 -> x0, waiting for transfers between devices: 23.6 us -> none  [body(): lax.all_gather(normed, 'batch', axis=0, tiled=True)]
    dot_general x2 -> x0, matrix products: 12.6 us -> none  [contract(): return jnp.dot(active, down_flat, preferred_element_type=jnp.float32)]
    slice x4 -> x0, local copies, waits for them, and re-layouts: 12.1 us -> none  [the longest x1 6.25 us: body(): down_part = down_recv[first_slot:first_slot + per_layer]]
    all_to_all x2 -> x0, starting transfers between devices: 10.5 us -> none  [the longest x1 5.24 us: body(): lax.all_to_all(down_send, 'owner', split_axis=0, concat_axis=0, tiled=True)]
    convert_element_type x4 -> x0, other arithmetic: 4.01 us -> none  [the longest x2 2.35 us: normalize(): (centered * lax.rsqrt(row_var + 1e-05) * gain_row[None, :]).astype(jnp.bf...]
  transfers between devices with their start and end apart: 6 -> 0, of which waited for: 5 -> 0; matrix products, arithmetic and copies ran while one was open for 8% -> 0% of each run, Pallas kernels for 0% -> 0%
where the time goes in v1:
time: 209 us; the launch traced here: 208 us
  Pallas kernels  191 us (91%)
  local copies, waits for them, and re-layouts  15.3 us (7%)
    pallas_call x2, Pallas kernels, run_layer(): pl.pallas_call(functools.partial(layer_kernel, layer_at, owners, batches)...  191 us
    gather x1, local copies, waits for them, and re-layouts, stay_body(): up_send = up_rows.reshape(held_blocks, BLOCK, model_width)[chosen]  6.56 us
    gather x1, local copies, waits for them, and re-layouts, stay_body(): down_send = down_rows.reshape(held_blocks, BLOCK, model_width)[chosen]  6.52 us

profile of v1, /device:TPU:0, one launch (start us, length us, event | category | flops | bytes accessed | tf_op | source)
XLA Modules:
  0.0 207.7 jit_solution(815399875212158374)
XLA Ops:
  0.0 0.9 fusion
  0.9 0.9 convert_reduce_fusion
  1.7 0.7 broadcast_in_dim.15.live_ref
  2.4 6.5 %gather_fusion.1 = bf16[4,128,6144]{2,1,0:T(8,128)(2,1)} fusion(bf16[24,128,6144]{2,1,0:T(8,128)(2,1)} %bitcast.2, s32[1024]{0:T(1024)S(1)} %pad_clamp_fusion), kind=kCustom, calls=%fused_computation.1 | custom fusion | bytes 12582928 | tf_op jit(solution)/shard_map/gather | solution.py:303
  8.9 6.6 %gather_fusion = bf16[4,128,6144]{2,1,0:T(8,128)(2,1)} fusion(bf16[24,128,6144]{2,1,0:T(8,128)(2,1)} %bitcast.3, s32[1024]{0:T(1024)S(1)} %pad_clamp_fusion), kind=kCustom, calls=%fused_computation | custom fusion | bytes 12582928 | tf_op jit(solution)/shard_map/gather | solution.py:302
  15.5 95.5 %sublayer_0.1.state_ref = bf16[16,6144]{1,0:T(8,128)(2,1)} custom-call(bf16[16,6144]{1,0:T(8,128)(2,1)} %state_ref.1, f32[2,6144]{1,0:T(2,128)} %gains_ref.3, f32[4,128]{1,0:T(4,128)} %broadcast_in_dim.15.live_ref, bf16[4,128,6144]{2,1,0:T(8,128)(2,1)} %gather_fusion, bf16[4,128,6144]{2,1,0:T(8,128)(2,1)} %gather_fusion.1), custom_call_target="tpu_custom_call" | custom-call | tf_op jit(solution)/shard_map/sublayer_0/pallas_call | solution.py:282
  111.0 95.1 %sublayer_1.1 = bf16[16,6144]{1,0:T(8,128)(2,1)} custom-call(bf16[16,6144]{1,0:T(8,128)(2,1)} %sublayer_0.1.state_ref, f32[2,6144]{1,0:T(2,128)} %gains_ref.3, f32[4,128]{1,0:T(4,128)} %broadcast_in_dim.15.live_ref, bf16[4,128,6144]{2,1,0:T(8,128)(2,1)} %gather_fusion, bf16[4,128,6144]{2,1,0:T(8,128)(2,1)} %gather_fusion.1), custom_call_target="tpu_custom_call" | custom-call | tf_op jit(solution)/shard_map/sublayer_1/pallas_call | solution.py:282
  206.1 1.6 copy.7
  (1 shorter events, 0.0 us)

commit v2 on v1

--- a/solution.py
+++ b/solution.py
@@ -88,7 +88,7 @@
             for h in range(2):
                 move(o, slot(at_z(k)), h, ps.at[o, k, h], p_dev).start()
 
-        for t in range(zn + 2):
+        for t in range(zn + 1):
             if t < zn:
                 b = slot(at_z(t))
                 if t > 0:
@@ -97,31 +97,22 @@
                 for h in range(2):
                     move(me_o, b, h, xs.at[t, h], x_dev).start()
                 to_partner(me_o, t)
-            if 1 <= t <= zn:
+            if t >= 1:
                 b = slot(at_z(t - 1))
-                for h in range(2):
+                for h in (1, 0):
                     arrive(peer_y, b, h)
-                move(peer_y, b, 1, x2s.at[t - 1], x_dev).start()
+                    if h == 1:
+                        move(peer_y, b, 1, x2s.at[t - 1], x_dev).start()
                 to_partner(peer_y, t - 1)
-            if t >= 2:
-                b = slot(at_z(t - 2))
-                for o in (peer_x, diag):
-                    for h in range(2):
-                        arrive(o, b, h)
-                    to_partner(o, t - 2)
-
-        for g in range(owners):
+
+        def give(g, k):
+            z = at_z(k)
+            return remote(part.at[g, z * CORES + (1 - core)], core_in.at[g, z], cs.at[g, k], cr.at[g, z], p_dev)
+
+        def group(g):
             for k in range(zn):
                 for h in range(2):
                     arrive(g, at_z(k) * CORES + (1 - core), h)
-        pltpu.make_async_copy(up_hbm, up_v, wsem.at[0]).wait()
-        pltpu.make_async_copy(down_hbm, down_v, wsem.at[1]).wait()
-
-        def give(g, k):
-            z = at_z(k)
-            return remote(part.at[g, z * CORES + (1 - core)], core_in.at[g, z], cs.at[g, k], cr.at[g, z], p_dev)
-
-        def group(g, carry):
             flat = acts[g].reshape(batches * rows, width)
             pre = lax.dot_general(flat, up_v[g], (((1,), (1,)), ((), ())), preferred_element_type=jnp.float32)
             active = (jnp.maximum(pre, 0.0) * live_ref[pl.ds(g, 1), :]).astype(jnp.bfloat16)
@@ -131,14 +122,21 @@
                 part[g, :, :, cols] = made.astype(jnp.bfloat16).reshape(batches, rows, -1)
             for k in range(zn):
                 give(g, k).start()
-            return carry
-
-        lax.fori_loop(0, owners, group, 0)
 
         def join(g, z, b):
             remote(part.at[g, b], core_in.at[g, z], cs.at[g, 0], cr.at[g, z], p_dev).wait_recv()
             core_in[g, z] = (core_in[g, z].astype(jnp.float32) + part[g, b].astype(jnp.float32)).astype(jnp.bfloat16)
 
+        pltpu.make_async_copy(up_hbm, up_v, wsem.at[0]).wait()
+        pltpu.make_async_copy(down_hbm, down_v, wsem.at[1]).wait()
+        group(me_o)
+        for k in range(zn):
+            for o in (diag, peer_x):
+                for h in range(2):
+                    arrive(o, slot(at_z(k)), h)
+                to_partner(o, k)
+        group(peer_y)
+        group(diag)
         h2 = pl.ds(half, half)
         h1 = pl.ds(0, half)
         for k in range(zn):
@@ -146,12 +144,9 @@
             join(diag, z, slot(z))
             remote(core_in.at[diag, z, :, h2], x2_in.at[z], rx2s.at[k], rx2r.at[z], x_dev).start()
             remote(core_in.at[diag, z, :, h1], relay_in.at[z], ryrs.at[k], ryrr.at[z], y_dev).start()
-        for k in range(zn):
-            z = at_z(k)
             join(peer_y, z, slot(z))
             remote(core_in.at[peer_y, z, :, h1], y_in.at[z, :, h1], rys.at[k, 0], ryr.at[z, 0], y_dev).start()
-            join(peer_x, z, slot(z))
-            remote(core_in.at[peer_x, z], x_in.at[z], rxs.at[k], rxr.at[z], x_dev).start()
+        group(peer_x)
         for k in range(zn):
             z = at_z(k)
             remote(core_in.at[diag, z, :, h2], x2_in.at[z], rx2s.at[k], rx2r.at[z], x_dev).wait_recv()
@@ -159,6 +154,10 @@
                 core_in[peer_y, z, :, half:].astype(jnp.float32) + x2_in[z].astype(jnp.float32)
             ).astype(jnp.bfloat16)
             remote(core_in.at[peer_y, z, :, h2], y_in.at[z, :, h2], rys.at[k, 1], ryr.at[z, 1], y_dev).start()
+        for k in list(range(1, zn)) + [0]:
+            z = at_z(k)
+            join(peer_x, z, slot(z))
+            remote(core_in.at[peer_x, z], x_in.at[z], rxs.at[k], rxr.at[z], x_dev).start()
         for k in list(range(1, zn)) + [0]:
             z = at_z(k)
             join(me_o, z, slot(z))
@@ -291,17 +290,55 @@
     )(state, gains, live, up_send, down_send)
 
 
+def fetch_kernel(owners, batches, held, pick_ref, up_ref, down_ref, live_ref, up_out, down_out, buf, isem, osem):
+    sender = lax.axis_index("owner") * batches + lax.axis_index("batch")
+
+    def read(i):
+        g = i % owners
+        at = jnp.minimum(pick_ref[g, sender], held - 1)
+        src = up_ref if i < owners else down_ref
+        return pltpu.make_async_copy(src.at[at], buf.at[i], isem.at[i])
+
+    def write(i):
+        dst = up_out if i < owners else down_out
+        return pltpu.make_async_copy(buf.at[i], dst.at[i % owners], osem.at[i])
+
+    for i in range(2 * owners):
+        read(i).start()
+    for g in range(owners):
+        live = (pick_ref[g, sender] < held).astype(jnp.float32)
+        live_ref[g:g + 1, :] = jnp.full((1, BLOCK), live, jnp.float32)
+    for i in range(2 * owners):
+        read(i).wait()
+        write(i).start()
+    for i in range(2 * owners):
+        write(i).wait()
+
+
+def fetch(owners, batches, up_rows, down_rows, pick):
+    width = up_rows.shape[1]
+    held = up_rows.shape[0] // BLOCK
+    hbm = pl.BlockSpec(memory_space=pl.ANY)
+    sent = jax.ShapeDtypeStruct((owners, BLOCK, width), up_rows.dtype)
+    return pl.pallas_call(
+        functools.partial(fetch_kernel, owners, batches, held),
+        out_shape=(jax.ShapeDtypeStruct((owners, BLOCK), jnp.float32), sent, sent),
+        in_specs=[pl.BlockSpec(memory_space=pltpu.SMEM), hbm, hbm],
+        out_specs=(pl.BlockSpec(memory_space=pltpu.VMEM), hbm, hbm),
+        scratch_shapes=[
+            pltpu.VMEM((2 * owners, BLOCK, width), up_rows.dtype),
+            pltpu.SemaphoreType.DMA((2 * owners,)),
+            pltpu.SemaphoreType.DMA((2 * owners,)),
+        ],
+        compiler_params=pltpu.CompilerParams(vmem_limit_bytes=VMEM_BUDGET),
+        name="fetch",
+    )(pick, up_rows.reshape(held, BLOCK, width), down_rows.reshape(held, BLOCK, width))
+
+
 def stay_body(hidden, gains, up_rows, down_rows, pick):
     owners = lax.axis_size("owner")
     batches = lax.axis_size("batch")
-    held_blocks = up_rows.shape[0] // BLOCK
-    model_width = up_rows.shape[1]
-    sender = lax.axis_index("owner") * batches + lax.axis_index("batch")
-    my_picks = lax.dynamic_slice_in_dim(pick, sender, 1, 1)[:, 0]
-    chosen = jnp.minimum(my_picks, held_blocks - 1)
-    up_send = up_rows.reshape(held_blocks, BLOCK, model_width)[chosen]
-    down_send = down_rows.reshape(held_blocks, BLOCK, model_width)[chosen]
-    live = jnp.broadcast_to((my_picks < held_blocks).astype(jnp.float32)[:, None], (owners, BLOCK))
+    live, up_send, down_send = fetch(owners, batches, up_rows, down_rows, pick)
     state = hidden
     for layer_at in range(LAYERS):
         state = run_layer(layer_at, owners, batches, state, gains, live, up_send, down_send)

time: 209 us -> 196 us (0.938)
  local copies, waits for them, and re-layouts: 15.3 us -> 1.62 us
  Pallas kernels: 191 us -> 194 us
    gather x2 -> x0, local copies, waits for them, and re-layouts: 13.1 us -> none  [the longest x1 6.56 us: stay_body(): up_send = up_rows.reshape(held_blocks, BLOCK, model_width)[chosen]]
    pallas_call x0 -> x1, Pallas kernels: none -> 10.4 us  [fetch(): pl.pallas_call(functools.partial(fetch_kernel, owners, batches, held), ou...]
    pallas_call x2, Pallas kernels: 191 us -> 184 us  [run_layer(): pl.pallas_call(functools.partial(layer_kernel, layer_at, owners, batches)...]
where the time goes in v2:
time: 196 us
  Pallas kernels  194 us (99%)
    pallas_call x2, Pallas kernels, run_layer(): pl.pallas_call(functools.partial(layer_kernel, layer_at, owners, batches)...  184 us
    pallas_call x1, Pallas kernels, fetch(): pl.pallas_call(functools.partial(fetch_kernel, owners, batches, held), ou...  10.4 us

profile of v2, /device:TPU:0, one launch (start us, length us, event | category | flops | bytes accessed | tf_op | source)
XLA Modules:
  0.0 195.7 jit_solution(10492572897270682454)
XLA Ops:
  0.0 10.4 %fetch.1 = (f32[4,128]{1,0:T(4,128)}, bf16[4,128,6144]{2,1,0:T(8,128)(2,1)}, bf16[4,128,6144]{2,1,0:T(8,128)(2,1)}) custom-call(s32[4,32]{1,0:T(4,128)} %pick_ref.1, bf16[24,128,6144]{2,1,0:T(8,128)(2,1)} %bitcast.2, bf16[24,128,6144]{2,1,0:T(8,128)(2,1)} %bitcast.3), custom_call_target="tpu_custom_call" | custom-call | tf_op jit(solution)/shard_map/fetch/pallas_call | solution.py:323
  10.5 87.4 %sublayer_0.1.state_ref = bf16[16,6144]{1,0:T(8,128)(2,1)} custom-call(bf16[16,6144]{1,0:T(8,128)(2,1)} %state_ref.1, f32[2,6144]{1,0:T(2,128)} %gains_ref.3, f32[4,128]{1,0:T(4,128)} %get-tuple-element.8.live_ref, bf16[4,128,6144]{2,1,0:T(8,128)(2,1)} %get-tuple-element.9.up_hbm, bf16[4,128,6144]{2,1,0:T(8,128)(2,1)} %get-tuple-element.10.down_hbm), custom_call_target="tpu_custom_call" | custom-call | tf_op jit(solution)/shard_map/sublayer_0/pallas_call | solution.py:281
  97.9 96.2 %sublayer_1.1 = bf16[16,6144]{1,0:T(8,128)(2,1)} custom-call(bf16[16,6144]{1,0:T(8,128)(2,1)} %sublayer_0.1.state_ref, f32[2,6144]{1,0:T(2,128)} %gains_ref.3, f32[4,128]{1,0:T(4,128)} %get-tuple-element.8.live_ref, bf16[4,128,6144]{2,1,0:T(8,128)(2,1)} %get-tuple-element.9.up_hbm, bf16[4,128,6144]{2,1,0:T(8,128)(2,1)} %get-tuple-element.10.down_hbm), custom_call_target="tpu_custom_call" | custom-call | tf_op jit(solution)/shard_map/sublayer_1/pallas_call | solution.py:281
  194.1 1.6 copy.7

commit v3 on v2

--- a/solution.py
+++ b/solution.py
@@ -37,7 +37,15 @@
     in_layer = hi == layer_at
 
     def at_z(k):
-        return (zi + k) % zn
+        if zn & (zn - 1):
+            return (zi + k) % zn
+        found, bit = 0, 1
+        while bit < zn:
+            found = found + ((zi // bit + k // bit) % 2) * bit
+            bit *= 2
+        return found
+
+    back = list(range(zn - 1, -1, -1))
 
     def z_dev(k):
         return (me_o, at_z(k) * CORES + core)
@@ -139,7 +147,7 @@
         group(diag)
         h2 = pl.ds(half, half)
         h1 = pl.ds(0, half)
-        for k in range(zn):
+        for k in back:
             z = at_z(k)
             join(diag, z, slot(z))
             remote(core_in.at[diag, z, :, h2], x2_in.at[z], rx2s.at[k], rx2r.at[z], x_dev).start()
@@ -147,18 +155,18 @@
             join(peer_y, z, slot(z))
             remote(core_in.at[peer_y, z, :, h1], y_in.at[z, :, h1], rys.at[k, 0], ryr.at[z, 0], y_dev).start()
         group(peer_x)
-        for k in range(zn):
+        for k in back:
             z = at_z(k)
             remote(core_in.at[diag, z, :, h2], x2_in.at[z], rx2s.at[k], rx2r.at[z], x_dev).wait_recv()
             core_in[peer_y, z, :, half:] = (
                 core_in[peer_y, z, :, half:].astype(jnp.float32) + x2_in[z].astype(jnp.float32)
             ).astype(jnp.bfloat16)
             remote(core_in.at[peer_y, z, :, h2], y_in.at[z, :, h2], rys.at[k, 1], ryr.at[z, 1], y_dev).start()
-        for k in list(range(1, zn)) + [0]:
+        for k in back:
             z = at_z(k)
             join(peer_x, z, slot(z))
             remote(core_in.at[peer_x, z], x_in.at[z], rxs.at[k], rxr.at[z], x_dev).start()
-        for k in list(range(1, zn)) + [0]:
+        for k in back:
             z = at_z(k)
             join(me_o, z, slot(z))
             remote(core_in.at[peer_x, z], x_in.at[z], rxs.at[k], rxr.at[z], x_dev).wait_recv()
@@ -204,12 +212,11 @@
         def pass_on(k, z):
             return remote(relay_in.at[z], x2_in.at[z], ryrs.at[k], rx2r.at[z], x_dev)
 
-        order = list(range(1, zn)) + [0]
-        for k in range(zn):
+        for k in back:
             z = at_z(k)
             remote(relay_in.at[z], relay_in.at[z], ryrs.at[k], ryrr.at[z], y_dev).wait_recv()
             pass_on(k, z).start()
-        for k in order:
+        for k in back:
             z = at_z(k)
             remote(y_in.at[z, :, h1], y_in.at[z, :, h1], rys.at[k, 0], ryr.at[z, 0], y_dev).wait_recv()
             pass_on(k, z).wait_recv()

time: 196 us -> 176 us (0.90)
  Pallas kernels: 194 us -> 173 us
    pallas_call x2, Pallas kernels: 184 us -> 162 us  [run_layer(): pl.pallas_call(functools.partial(layer_kernel, layer_at, owners, batches)...]
where the time goes in v3:
time: 176 us; the launch traced here: 175 us
  Pallas kernels  173 us (98%)
    pallas_call x2, Pallas kernels, run_layer(): pl.pallas_call(functools.partial(layer_kernel, layer_at, owners, batches)...  162 us
    pallas_call x1, Pallas kernels, fetch(): pl.pallas_call(functools.partial(fetch_kernel, owners, batches, held), ou...  10.6 us

profile of v3, /device:TPU:0, one launch (start us, length us, event | category | flops | bytes accessed | tf_op | source)
XLA Modules:
  0.0 174.7 jit_solution(15976886940391750795)
XLA Ops:
  0.0 10.6 %fetch.1 = (f32[4,128]{1,0:T(4,128)}, bf16[4,128,6144]{2,1,0:T(8,128)(2,1)}, bf16[4,128,6144]{2,1,0:T(8,128)(2,1)}) custom-call(s32[4,32]{1,0:T(4,128)} %pick_ref.1, bf16[24,128,6144]{2,1,0:T(8,128)(2,1)} %bitcast.2, bf16[24,128,6144]{2,1,0:T(8,128)(2,1)} %bitcast.3), custom_call_target="tpu_custom_call" | custom-call | tf_op jit(solution)/shard_map/fetch/pallas_call | solution.py:330
  10.6 79.6 %sublayer_0.1.state_ref = bf16[16,6144]{1,0:T(8,128)(2,1)} custom-call(bf16[16,6144]{1,0:T(8,128)(2,1)} %state_ref.1, f32[2,6144]{1,0:T(2,128)} %gains_ref.3, f32[4,128]{1,0:T(4,128)} %get-tuple-element.8.live_ref, bf16[4,128,6144]{2,1,0:T(8,128)(2,1)} %get-tuple-element.9.up_hbm, bf16[4,128,6144]{2,1,0:T(8,128)(2,1)} %get-tuple-element.10.down_hbm), custom_call_target="tpu_custom_call" | custom-call | tf_op jit(solution)/shard_map/sublayer_0/pallas_call | solution.py:288
  90.2 82.9 %sublayer_1.1 = bf16[16,6144]{1,0:T(8,128)(2,1)} custom-call(bf16[16,6144]{1,0:T(8,128)(2,1)} %sublayer_0.1.state_ref, f32[2,6144]{1,0:T(2,128)} %gains_ref.3, f32[4,128]{1,0:T(4,128)} %get-tuple-element.8.live_ref, bf16[4,128,6144]{2,1,0:T(8,128)(2,1)} %get-tuple-element.9.up_hbm, bf16[4,128,6144]{2,1,0:T(8,128)(2,1)} %get-tuple-element.10.down_hbm), custom_call_target="tpu_custom_call" | custom-call | tf_op jit(solution)/shard_map/sublayer_1/pallas_call | solution.py:288
  173.0 1.6 copy.7
